TPU v7x, 32 devices: a whole 2x2x4 slice. The times are simulated.
32 devices in a mesh: col: 2 (over core), dev: 16 (over z, y, x).
Axes of the slice: x: 2, y: 2, z: 4, core: 2. Of those that a mesh axis runs over, the one named last changes fastest.
Arguments:
- factor_a: float32 [1536, 16, 512], P('dev'), may hold values from -1 to 1
- factor_b: float32 [1536, 64, 512], P('dev', 'col'), may hold values from -1 to 1
- factor_occ: float32 [1536, 16, 512], P('dev'), may hold values from -1 to 1
- singles_a: float32 [16, 16], replicated, may hold values from -1.5 to 1.5
- singles_b: float32 [16, 64], P(None, 'col'), may hold values from -1.5 to 1.5
- doubles: bfloat16 [512, 512, 256], P('col', 'dev'), may hold values from -0.023925781 to 0.023925781
- orbital_a: float32 [16], P('col'), may hold values from 0.2 to 3
- orbital_b: float32 [64], P('dev'), may hold values from 0.2 to 3
- orbital_occ: float32 [16], replicated, may hold values from -2 to -0.3
Outputs:
- update: float32 [16, 64, 256], P('col', 'dev')
All inputs are finite; a program needn't handle non-finite values.
Results may differ from a plain program's by a relative error of at most 0.0049.
Values may be sent and summed in bfloat16 or wider, within the bound.
No kernel may reach another device: no remote copies, remote signals or barrier semaphores. Data moves between devices by JAX's collectives and lax.ppermute only.
A program may use at most 128 MiB of HBM per device.

v0:
```python
import jax
import jax.numpy as jnp
from jax import lax
from jax.sharding import PartitionSpec as P


def body(
    factor_a, factor_b, factor_occ, singles_a, singles_b, doubles, orbital_a, orbital_b, orbital_occ
):
    highest = lax.Precision.HIGHEST
    c_tile = doubles.shape[0]
    d_tile = doubles.shape[1]
    pair_count = doubles.shape[2]
    shard_rows = factor_a.shape[0]
    a_rows = factor_a.shape[1]
    b_local = factor_b.shape[1]
    d_groups = factor_b.shape[2] // d_tile
    col_index = lax.axis_index("col")
    occ_tile = lax.dynamic_slice_in_dim(factor_occ, col_index * c_tile, c_tile, 2)
    a_tile = lax.dynamic_slice_in_dim(factor_a, col_index * c_tile, c_tile, 2)
    dressed_a = (a_tile - jnp.einsum("ka,qkc->qac", singles_a, occ_tile, precision=highest)).astype(
        jnp.bfloat16
    )
    dressed_a = dressed_a.reshape(shard_rows, a_rows * c_tile)
    dressed_b = (
        factor_b - jnp.einsum("kb,qkd->qbd", singles_b, factor_occ, precision=highest)
    ).astype(jnp.bfloat16)
    grouped = dressed_b.reshape(shard_rows, b_local, d_groups, d_tile)
    grouped = jnp.transpose(grouped, (0, 2, 1, 3)).reshape(shard_rows, d_groups, b_local * d_tile)
    moved = lax.all_to_all(grouped, "dev", split_axis=1, concat_axis=0, tiled=True)
    collected = lax.all_gather(moved, "col", axis=1, tiled=True)
    whole_b = collected.reshape(collected.shape[0], -1)
    b_rows_all = whole_b.shape[1] // d_tile
    contract_first = (((0,), (0,)), ((), ()))
    whole_a = lax.all_gather(dressed_a, "dev", axis=0, tiled=True)
    integral = lax.dot_general(whole_a, whole_b, contract_first, preferred_element_type=jnp.float32)
    integral = integral.astype(jnp.bfloat16).reshape(a_rows, c_tile, b_rows_all, d_tile)
    integral = jnp.transpose(integral, (0, 2, 1, 3)).reshape(a_rows * b_rows_all, c_tile * d_tile)
    partial_value = jnp.dot(
        integral, doubles.reshape(c_tile * d_tile, pair_count), preferred_element_type=jnp.float32
    )
    partial_value = partial_value.reshape(a_rows, b_rows_all, pair_count)
    reduced = lax.psum_scatter(partial_value, "dev", scatter_dimension=1, tiled=True)
    total = lax.psum_scatter(reduced, "col", scatter_dimension=0, tiled=True)
    pair_energy = (orbital_occ[:, None] + orbital_occ[None, :]).reshape(-1)
    denominator = orbital_a[:, None, None] + orbital_b[None, :, None] - pair_energy[None, None, :]
    return total / denominator


def solution(mesh):
    return jax.shard_map(
        body,
        mesh=mesh,
        in_specs=(
            P("dev", None, None),
            P("dev", "col", None),
            P("dev", None, None),
            P(),
            P(None, "col"),
            P("col", "dev", None),
            P("col"),
            P("dev"),
            P(),
        ),
        out_specs=P("col", "dev", None),
        check_vma=False,
    )
```

profile of v0, /device:TPU:0, one launch (start us, length us, event | category | flops | bytes accessed | tf_op | source)
XLA Modules:
  0.0 448.8 jit_solution(5826299409805732357)
XLA Ops:
  6.5 0.0 copy-start
  6.5 0.0 all-gather.5.cloned.1.call-start
  6.5 1.9 copy-done
  8.4 8.8 %fusion.2 = bf16[96,32,512]{2,1,0:T(8,128)(2,1)} fusion(f32[96,32,512]{2,1,0:T(8,128)} %param.10, f32[96,16,512]{2,1,0:T(8,128)S(1)} %copy-done, f32[16,32]{1,0:T(8,128)} %param.13), kind=kOutput, calls=%fused_computation.4 | convolution fusion | flops 305135616 | bytes 12584960 | tf_op jit(solution)/shard_map/kb,qkd->qbd/dot_general | solution.py:26
  17.2 7.4 %copy.29 = bf16[96,32,512]{0,2,1:T(8,128)(2,1)} copy(bf16[96,32,512]{2,1,0:T(8,128)(2,1)} %fusion.2) | data formatting | bytes 6291456 | tf_op jit(solution)/shard_map/convert_element_type | solution.py:27
  24.6 5.3 %copy.30 = bf16[96,16,32,32]{0,3,2,1:T(8,128)(2,1)} copy(bf16[96,16,32,32]{0,3,1,2:T(8,128)(2,1)} %bitcast.48) | data formatting | bytes 6291456 | tf_op jit(solution)/shard_map/transpose | solution.py:29
  29.8 6.0 %copy.31 = bf16[96,16,1024]{2,0,1:T(8,128)(2,1)} copy(bf16[96,16,1024]{0,2,1:T(8,128)(2,1)} %bitcast.49) | data formatting | bytes 6291456 | tf_op jit(solution)/shard_map/reshape | solution.py:29
  35.9 0.0 copy-start.2
  35.9 79.8 %all_to_all.18 = bf16[96,16,1024]{2,0,1:T(8,128)(2,1)} all-to-all(bf16[96,16,1024]{2,0,1:T(8,128)(2,1)} %copy.31), channel_id=1, replica_groups=mesh['col'=2,'dev'=16] {'dev'}, dimensions={1} | all-to-all | bytes 6291456 | tf_op jit(solution)/shard_map/all_to_all | solution.py:30
  115.7 0.0 all-gather.5.cloned.1.call-update
  115.7 0.0 all-gather.3.cloned.1.call-start
  115.8 0.0 copy-done.2
  115.8 2.9 fusion.5
  118.7 1.2 copy.39
  119.9 0.0 all-gather.3.cloned.1.call-update
  119.9 0.2 reduce-scatter.3.cloned.1.call-start
  120.2 10.8 %all-gather.5.cloned.1.call-done = bf16[1536,2,1024]{2,0,1:T(8,128)(2,1)} async-done(((bf16[1536,1,1024]{2,0,1:T(8,128)(2,1)}), bf16[1536,2,1024]{2,0,1:T(8,128)(2,1)}) %all-gather.5.cloned.1.call-update) | async-done | bytes 6291472 | tf_op jit(solution)/shard_map/all_gather | solution.py:31
  131.0 8.7 %copy.32 = bf16[1536,2,1024]{0,2,1:T(8,128)(2,1)} copy(bf16[1536,2,1024]{2,0,1:T(8,128)(2,1)} %all-gather.5.cloned.1.call-done) | data formatting | bytes 12582912 | tf_op jit(solution)/shard_map/all_gather | solution.py:31
  139.6 146.7 %all-gather.3.cloned.1.call-done = bf16[1536,4096]{1,0:T(8,128)(2,1)} async-done(((bf16[96,4096]{1,0:T(8,128)(2,1)}), bf16[1536,4096]{1,0:T(8,128)(2,1)}) %all-gather.3.cloned.1.call-update) | async-done | bytes 12582928 | tf_op jit(solution)/shard_map/all_gather | solution.py:35
  286.4 32.6 %convolution_convert_fusion = bf16[4096,2048]{1,0:T(8,128)(2,1)} fusion(bf16[1536,4096]{1,0:T(8,128)(2,1)} %all-gather.3.cloned.1.call-done, bf16[1536,2048]{0,1:T(8,128)(2,1)} %bitcast.52), kind=kOutput, calls=%fused_computation.2 | convolution fusion | flops 25778192384 | bytes 35651584 | tf_op jit(solution)/shard_map/dot_general | solution.py:36
  318.9 21.4 %copy.33 = bf16[4096,2048]{0,1:T(8,128)(2,1)} copy(bf16[4096,2048]{1,0:T(8,128)(2,1)} %convolution_convert_fusion) | data formatting | bytes 33554432 | tf_op jit(solution)/shard_map/convert_element_type | solution.py:37
  340.3 0.0 copy-start.6
  340.3 10.7 %copy.40 = bf16[256,8,16,256]{3,2,1,0:T(8,128)(2,1)S(1)} copy(bf16[256,8,16,256]{3,1,2,0:T(8,128)(2,1)} %bitcast.47) | data formatting | bytes 33554432
  351.0 0.0 copy-done.6
  351.0 0.0 copy-start.3
  351.0 0.0 copy-start.4
  351.1 0.0 copy-start.5
  351.1 0.0 copy-start.1
  351.1 6.7 %fusion.10 = f32[16,64,256]{2,0,1:T(8,128)} fusion(bf16[256,32,256]{2,1,0:T(8,128)(2,1)S(1)} %copy-done.6, bf16[16,256,64,32]{1,0,3,2:T(8,128)(2,1)S(1)} %bitcast.50), kind=kOutput, calls=%fused_computation.11 | convolution fusion | flops 4294967296 | bytes 22020096 | tf_op jit(solution)/shard_map/dot_general | solution.py:39
  357.8 0.0 reduce-scatter.3.cloned.1.call-update
  357.8 0.0 reduce-scatter.5.cloned.1.call-start
  357.9 0.0 copy-done.3
  357.9 0.1 broadcast_add_fusion
  358.0 0.1 add.53
  358.0 76.8 %reduce-scatter.3.cloned.1.call-done = f32[16,4,256]{2,0,1:T(8,128)} async-done(((f32[16,64,256]{2,0,1:T(8,128)}), f32[16,4,256]{2,0,1:T(8,128)}) %reduce-scatter.3.cloned.1.call-update) | async-done | bytes 65552 | tf_op jit(solution)/shard_map/reduce_scatter | solution.py:43
  434.9 0.0 reduce-scatter.5.cloned.1.call-update
  434.9 0.0 copy-done.4
  434.9 0.0 copy-done.5
  434.9 0.1 broadcast_add_fusion.1
  435.0 5.8 %reduce-scatter.5.cloned.1.call-done = f32[8,4,256]{2,0,1:T(8,128)} async-done(((f32[16,4,256]{2,0,1:T(8,128)}), f32[8,4,256]{2,0,1:T(8,128)}) %reduce-scatter.5.cloned.1.call-update) | async-done | bytes 32784 | tf_op jit(solution)/shard_map/reduce_scatter | solution.py:44
  440.8 0.8 subtract_divide_fusion
  441.6 0.6 copy.35
  442.3 0.0 copy-done.1
Async XLA Ops:
  6.5 1.9 copy-start
  6.5 124.4 %all-gather.5.cloned.1.call-start = ((), (), s32[]{:S(2)}) async-start(), calls=%async_computation.4 | async-start | bytes 9437184 | tf_op jit(solution)/shard_map/all_gather | solution.py:31
  35.9 79.9 %copy-start.2 = (f32[16,16]{1,0:T(8,128)S(1)}, f32[16,16]{1,0:T(8,128)}, u32[]{:S(2)}) copy-start(f32[16,16]{1,0:T(8,128)} %param.12) | copy-start | bytes 3076
  115.7 170.6 %all-gather.3.cloned.1.call-start = ((), (), s32[]{:S(2)}) async-start(), calls=%async_computation.3 | async-start | bytes 13369344 | tf_op jit(solution)/shard_map/all_gather | solution.py:35
  119.9 314.9 %reduce-scatter.3.cloned.1.call-start = ((), (), s32[]{:S(2)}) async-start(), calls=%async_computation.5 | async-start | bytes 1114112 | tf_op jit(solution)/shard_map/reduce_scatter | solution.py:43
  340.3 10.7 %copy-start.6 = (bf16[256,32,256]{2,1,0:T(8,128)(2,1)S(1)}, bf16[256,32,256]{2,1,0:T(8,128)(2,1)}, u32[]{:S(2)}) copy-start(bf16[256,32,256]{2,1,0:T(8,128)(2,1)} %param.14) | copy-start | bytes 12582916
  351.0 6.8 %copy-start.3 = (f32[16]{0:T(128)S(1)}, f32[16]{0:T(128)}, u32[]{:S(2)}) copy-start(f32[16]{0:T(128)} %param.17) | copy-start | bytes 196
  351.0 83.8 %copy-start.4 = (f32[4]{0:T(128)S(1)}, f32[4]{0:T(128)}, u32[]{:S(2)}) copy-start(f32[4]{0:T(128)} %param.16) | copy-start | bytes 52
  351.1 83.8 %copy-start.5 = (f32[8]{0:T(128)S(1)}, f32[8]{0:T(128)}, u32[]{:S(2)}) copy-start(f32[8]{0:T(128)} %param.15) | copy-start | bytes 100
  351.1 91.2 %copy-start.1 = (f32[96,16,512]{2,1,0:T(8,128)S(1)}, f32[96,16,512]{2,1,0:T(8,128)}, u32[]{:S(2)}) copy-start(f32[96,16,512]{2,1,0:T(8,128)} %param.11) | copy-start | bytes 9437188
  357.8 83.0 %reduce-scatter.5.cloned.1.call-start = ((), (), s32[]{:S(2)}) async-start(), calls=%async_computation.6 | async-start | bytes 98304 | tf_op jit(solution)/shard_map/reduce_scatter | solution.py:44
Sparse Core Ops, SparseCore 0:
  115.8 15.0 all-gather.4
  133.7 152.5 all-gather.2
  357.9 76.8 reduce-scatter.2
  436.9 3.8 reduce-scatter.4
where the time goes:
time: 450 us; the launch traced here: 449 us
  waiting for transfers between devices  240 us (53%)
  blocking collectives  79.8 us (18%)
  local copies, waits for them, and re-layouts  63.3 us (14%)
  matrix products  51 us (11%)
  between operations  13.2 us (3%)
    all_gather x1, waiting for transfers between devices, body(): whole_a = lax.all_gather(dressed_a, 'dev', axis=0, tiled=True)  147 us
    all_to_all x1, blocking collectives, body(): lax.all_to_all(grouped, 'dev', split_axis=1, concat_axis=0, tiled=True)  79.8 us
    reduce_scatter x1, waiting for transfers between devices, body(): lax.psum_scatter(partial_value, 'dev', scatter_dimension=1, tiled=True)  76.8 us
    dot_general x1, matrix products, body(): lax.dot_general(whole_a, whole_b, contract_first, preferred_element_type=...  32.6 us
    convert_element_type x1, local copies, waits for them, and re-layouts, body(): integral.astype(jnp.bfloat16).reshape(a_rows, c_tile, b_rows_all, d_tile)  21.4 us
    unnamed x16, local copies, waits for them, and re-layouts  13.8 us
    all_gather x1, waiting for transfers between devices, body(): collected = lax.all_gather(moved, 'col', axis=1, tiled=True)  10.8 us
  transfers between devices with their start and end apart: 4, of which 4 were waited for; matrix products, arithmetic and copies ran while one was open for 3% of the time, Pallas kernels for 0%

commit v1 on v0

--- a/solution.py
+++ b/solution.py
@@ -32,7 +32,16 @@
     whole_b = collected.reshape(collected.shape[0], -1)
     b_rows_all = whole_b.shape[1] // d_tile
     contract_first = (((0,), (0,)), ((), ()))
-    whole_a = lax.all_gather(dressed_a, "dev", axis=0, tiled=True)
+    ways = lax.axis_size("dev")
+    up = [(d, (d + 1) % ways) for d in range(ways)]
+    down = [(d, (d - 1) % ways) for d in range(ways)]
+    earlier, later = ([dressed_a], [dressed_a])
+    for _ in range(ways // 2):
+        earlier.append(lax.ppermute(earlier[-1], "dev", up))
+    for _ in range((ways - 1) // 2):
+        later.append(lax.ppermute(later[-1], "dev", down))
+    line = jnp.concatenate([*earlier[::-1], *later[1:]], axis=0)
+    whole_a = jnp.roll(line, (lax.axis_index("dev") - ways // 2) * dressed_a.shape[0], axis=0)
     integral = lax.dot_general(whole_a, whole_b, contract_first, preferred_element_type=jnp.float32)
     integral = integral.astype(jnp.bfloat16).reshape(a_rows, c_tile, b_rows_all, d_tile)
     integral = jnp.transpose(integral, (0, 2, 1, 3)).reshape(a_rows * b_rows_all, c_tile * d_tile)

time: 450 us -> 579 us (1.29)
  blocking collectives: 79.8 us -> 0 us
  waiting for transfers between devices: 240 us -> 319 us
  starting transfers between devices: 0.31 us -> 67.1 us
  local copies, waits for them, and re-layouts: 63.3 us -> 125 us
    ppermute x0 -> x15, waiting for transfers between devices: none -> 210 us  [the longest x8 144 us: body(): earlier.append(lax.ppermute(earlier[-1], 'dev', up))]
    all_gather x1 -> x0, waiting for transfers between devices: 147 us -> none  [body(): whole_a = lax.all_gather(dressed_a, 'dev', axis=0, tiled=True)]
    all_to_all x1 -> x0, blocking collectives: 79.8 us -> none  [body(): lax.all_to_all(grouped, 'dev', split_axis=1, concat_axis=0, tiled=True)]
    ppermute x0 -> x15, starting transfers between devices: none -> 60.9 us  [the longest x8 51.9 us: body(): earlier.append(lax.ppermute(earlier[-1], 'dev', up))]
    unnamed x16 -> x83, local copies, waits for them, and re-layouts: 13.8 us -> 73.8 us
    reduce_scatter x1, waiting for transfers between devices: 76.8 us -> 102 us  [body(): lax.psum_scatter(partial_value, 'dev', scatter_dimension=1, tiled=True)]
    all_gather x1, waiting for transfers between devices: 10.8 us -> 0.01 us  [body(): collected = lax.all_gather(moved, 'col', axis=1, tiled=True)]
    all_to_all x0 -> x1, starting transfers between devices: none -> 5.94 us  [body(): lax.all_to_all(grouped, 'dev', split_axis=1, concat_axis=0, tiled=True)]
  transfers between devices with their start and end apart: 4 -> 19, of which waited for: 4 -> 14; matrix products, arithmetic and copies ran while one was open for 3% -> 15% of each run, Pallas kernels for 0% -> 0%
where the time goes in v1:
time: 579 us; the launch traced here: 576 us
  waiting for transfers between devices  319 us (55%)
  local copies, waits for them, and re-layouts  125 us (22%)
  starting transfers between devices  67.1 us (12%)
  matrix products  51.1 us (9%)
  between operations  13.4 us (2%)
    ppermute x8, waiting for transfers between devices, body(): earlier.append(lax.ppermute(earlier[-1], 'dev', up))  144 us
    reduce_scatter x1, waiting for transfers between devices, body(): lax.psum_scatter(partial_value, 'dev', scatter_dimension=1, tiled=True)  102 us
    unnamed x83, local copies, waits for them, and re-layouts  73.8 us
    ppermute x7, waiting for transfers between devices, body(): later.append(lax.ppermute(later[-1], 'dev', down))  65.9 us
    ppermute x8, starting transfers between devices, body(): earlier.append(lax.ppermute(earlier[-1], 'dev', up))  51.9 us
    dot_general x1, matrix products, body(): lax.dot_general(whole_a, whole_b, contract_first, preferred_element_type=...  32.7 us
    convert_element_type x1, local copies, waits for them, and re-layouts, body(): integral.astype(jnp.bfloat16).reshape(a_rows, c_tile, b_rows_all, d_tile)  20.7 us
  transfers between devices with their start and end apart: 19, of which 14 were waited for; matrix products, arithmetic and copies ran while one was open for 15% of the time, Pallas kernels for 0%

profile of v1, /device:TPU:0, one launch (start us, length us, event | category | flops | bytes accessed | tf_op | source)
XLA Modules:
  0.0 576.3 jit_solution(8490889482776840341)
XLA Ops:
  6.5 1.9 copy-done
  8.4 2.9 fusion.6
  11.4 1.2 copy.39
  12.6 3.0 collective-permute-start
  15.5 8.8 %fusion.3 = bf16[96,32,512]{2,1,0:T(8,128)(2,1)} fusion(f32[96,32,512]{2,1,0:T(8,128)} %param.10, f32[96,16,512]{2,1,0:T(8,128)S(1)} %copy-done, f32[16,32]{1,0:T(8,128)} %param.13), kind=kOutput, calls=%fused_computation.5 | convolution fusion | flops 305135616 | bytes 12584960 | tf_op jit(solution)/shard_map/kb,qkd->qbd/dot_general | solution.py:26
  24.3 7.4 %copy.29 = bf16[96,32,512]{0,2,1:T(8,128)(2,1)} copy(bf16[96,32,512]{2,1,0:T(8,128)(2,1)} %fusion.3) | data formatting | bytes 6291456 | tf_op jit(solution)/shard_map/convert_element_type | solution.py:27
  31.7 5.3 copy.30
  37.0 6.0 %copy.31 = bf16[96,16,1024]{2,0,1:T(8,128)(2,1)} copy(bf16[96,16,1024]{0,2,1:T(8,128)(2,1)} %bitcast.48) | data formatting | bytes 6291456 | tf_op jit(solution)/shard_map/reshape | solution.py:29
  43.0 5.9 %all-to-all-start = ((bf16[96,16,1024]{2,0,1:T(8,128)(2,1)}), bf16[96,16,1024]{2,0,1:T(8,128)(2,1)S(1)}, u32[]{:S(2)}, u32[]{:S(2)}) async-start(bf16[96,16,1024]{2,0,1:T(8,128)(2,1)} %copy.31), calls=%async_computation | async-start | bytes 6291456 | tf_op jit(solution)/shard_map/all_to_all | solution.py:30
  49.0 2.0 collective-permute-start.1
  51.0 3.7 collective-permute-start.8
  54.7 68.8 %collective-permute-done.1 = bf16[96,4096]{1,0:T(8,128)(2,1)S(1)} collective-permute-done((bf16[96,4096]{1,0:T(8,128)(2,1)}, bf16[96,4096]{1,0:T(8,128)(2,1)S(1)}, u32[]{:S(2)}, u32[]{:S(2)}) %collective-permute-start.1) | collective-permute-done | bytes 786464 | tf_op jit(solution)/shard_map/ppermute | solution.py:40
  123.5 2.8 collective-permute-done.8
  127.2 2.9 collective-permute-start.9
  130.1 26.0 %collective-permute-done.2 = bf16[96,4096]{1,0:T(8,128)(2,1)S(1)} collective-permute-done((bf16[96,4096]{1,0:T(8,128)(2,1)S(1)}, bf16[96,4096]{1,0:T(8,128)(2,1)S(1)}, u32[]{:S(2)}, u32[]{:S(2)}) %collective-permute-start.2) | collective-permute-done | bytes 786464 | tf_op jit(solution)/shard_map/ppermute | solution.py:40
  156.1 2.5 collective-permute-start.3
  159.4 2.4 collective-permute-start.10
  161.8 15.3 %collective-permute-done.3 = bf16[96,4096]{1,0:T(8,128)(2,1)S(1)} collective-permute-done((bf16[96,4096]{1,0:T(8,128)(2,1)S(1)}, bf16[96,4096]{1,0:T(8,128)(2,1)S(1)}, u32[]{:S(2)}, u32[]{:S(2)}) %collective-permute-start.3) | collective-permute-done | bytes 786464 | tf_op jit(solution)/shard_map/ppermute | solution.py:40
  177.1 14.9 %collective-permute-done.10 = bf16[96,4096]{1,0:T(8,128)(2,1)S(1)} collective-permute-done((bf16[96,4096]{1,0:T(8,128)(2,1)S(1)}, bf16[96,4096]{1,0:T(8,128)(2,1)S(1)}, u32[]{:S(2)}, u32[]{:S(2)}) %collective-permute-start.10) | collective-permute-done | bytes 786464 | tf_op jit(solution)/shard_map/ppermute | solution.py:42
  193.0 4.2 collective-permute-done.4
  197.2 22.0 %collective-permute-start.5 = (bf16[96,4096]{1,0:T(8,128)(2,1)S(1)}, bf16[96,4096]{1,0:T(8,128)(2,1)S(1)}, u32[]{:S(2)}, u32[]{:S(2)}) collective-permute-start(bf16[96,4096]{1,0:T(8,128)(2,1)S(1)} %collective-permute-done.4), channel_id=1, source_target_pairs={{0,1},{1,2},{2,3},{3,4},{4,5},{5,6},{6,7},{7,8},{8,9},{9,10},{10,1... | collective-permute-start | bytes 2359304 | tf_op jit(solution)/shard_map/ppermute | solution.py:40
  219.2 15.9 %collective-permute-done.11 = bf16[96,4096]{1,0:T(8,128)(2,1)S(1)} collective-permute-done((bf16[96,4096]{1,0:T(8,128)(2,1)S(1)}, bf16[96,4096]{1,0:T(8,128)(2,1)S(1)}, u32[]{:S(2)}, u32[]{:S(2)}) %collective-permute-start.11) | collective-permute-done | bytes 786464 | tf_op jit(solution)/shard_map/ppermute | solution.py:42
  235.9 15.9 %collective-permute-done.5 = bf16[96,4096]{1,0:T(8,128)(2,1)S(1)} collective-permute-done((bf16[96,4096]{1,0:T(8,128)(2,1)S(1)}, bf16[96,4096]{1,0:T(8,128)(2,1)S(1)}, u32[]{:S(2)}, u32[]{:S(2)}) %collective-permute-start.5) | collective-permute-done | bytes 786464 | tf_op jit(solution)/shard_map/ppermute | solution.py:40
  251.7 2.7 collective-permute-start.6
  254.4 16.5 %collective-permute-done.12 = bf16[96,4096]{1,0:T(8,128)(2,1)} collective-permute-done((bf16[96,4096]{1,0:T(8,128)(2,1)S(1)}, bf16[96,4096]{1,0:T(8,128)(2,1)}, u32[]{:S(2)}, u32[]{:S(2)}) %collective-permute-start.12) | collective-permute-done | bytes 786464 | tf_op jit(solution)/shard_map/ppermute | solution.py:42
  271.0 19.9 %collective-permute-start.7 = (bf16[96,4096]{1,0:T(8,128)(2,1)}, bf16[96,4096]{1,0:T(8,128)(2,1)}, u32[]{:S(2)}, u32[]{:S(2)}) collective-permute-start(bf16[96,4096]{1,0:T(8,128)(2,1)} %collective-permute-done.6), channel_id=1, source_target_pairs={{0,1},{1,2},{2,3},{3,4},{4,5},{5,6},{6,7},{7,8},{8,9},{9,10},{10,1... | collective-permute-start | bytes 2359304 | tf_op jit(solution)/shard_map/ppermute | solution.py:40
  290.9 15.0 %collective-permute-done.13 = bf16[96,4096]{1,0:T(8,128)(2,1)} collective-permute-done((bf16[96,4096]{1,0:T(8,128)(2,1)}, bf16[96,4096]{1,0:T(8,128)(2,1)}, u32[]{:S(2)}, u32[]{:S(2)}) %collective-permute-start.13) | collective-permute-done | bytes 786464 | tf_op jit(solution)/shard_map/ppermute | solution.py:42
  305.9 1.6 copy-done.2
  307.9 14.2 %collective-permute-done.7 = bf16[96,4096]{1,0:T(8,128)(2,1)} collective-permute-done((bf16[96,4096]{1,0:T(8,128)(2,1)}, bf16[96,4096]{1,0:T(8,128)(2,1)}, u32[]{:S(2)}, u32[]{:S(2)}) %collective-permute-start.7) | collective-permute-done | bytes 786464 | tf_op jit(solution)/shard_map/ppermute | solution.py:40
  322.1 2.1 constant_dynamic-update-slice_fusion.31
  324.2 2.1 constant_dynamic-update-slice_fusion.30
  326.2 2.1 constant_dynamic-update-slice_fusion.29
  328.3 2.1 constant_dynamic-update-slice_fusion.28
  330.4 2.1 constant_dynamic-update-slice_fusion.27
  332.4 2.1 constant_dynamic-update-slice_fusion.26
  334.5 2.1 constant_dynamic-update-slice_fusion.25
  336.6 2.1 constant_dynamic-update-slice_fusion.24
  338.7 2.1 constant_dynamic-update-slice_fusion.23
  340.7 2.2 constant_dynamic-update-slice_fusion.22
  343.0 2.3 constant_dynamic-update-slice_fusion.21
  345.2 2.1 constant_dynamic-update-slice_fusion.20
  347.4 2.1 constant_dynamic-update-slice_fusion.19
  349.5 2.1 constant_dynamic-update-slice_fusion.18
  351.6 2.1 constant_dynamic-update-slice_fusion.17
  353.7 2.1 constant_dynamic-update-slice_fusion.16
  355.8 2.1 constant_dynamic-update-slice_fusion.15
  357.8 2.1 constant_dynamic-update-slice_fusion.14
  360.8 1.0 constant_dynamic-update-slice_fusion.12
  361.8 1.0 constant_dynamic-update-slice_fusion.11
  363.7 1.0 constant_dynamic-update-slice_fusion.9
  364.7 2.1 constant_dynamic-update-slice_fusion.8
  366.8 2.1 constant_dynamic-update-slice_fusion.7
  370.8 1.0 constant_dynamic-update-slice_fusion.4
  371.7 1.0 constant_dynamic-update-slice_fusion.3
  372.7 2.1 constant_dynamic-update-slice_fusion.2
  374.8 2.1 constant_dynamic-update-slice_fusion.1
  376.8 2.1 constant_dynamic-update-slice_fusion
  378.9 8.6 %copy.32 = bf16[1536,2,1024]{0,2,1:T(8,128)(2,1)} copy(bf16[1536,2,1024]{2,0,1:T(8,128)(2,1)} %all-gather.2.cloned.1.call-done) | data formatting | bytes 12582912 | tf_op jit(solution)/shard_map/all_gather | solution.py:31
  387.6 32.7 %convolution_convert_fusion = bf16[4096,2048]{1,0:T(8,128)(2,1)} fusion(bf16[1536,2048]{0,1:T(8,128)(2,1)} %bitcast.51, bf16[3072,4096]{1,0:T(8,128)(2,1)} %constant_dynamic-update-slice_fusion, s32[]{:T(128)S(6)} %select_n.19), kind=kOutput, calls=%fused_computation.2 | convolution fusion | flops 25778192384 | bytes 35651588 | tf_op jit(solution)/shard_map/dot_general | solution.py:45
  420.2 20.7 %copy.33 = bf16[4096,2048]{0,1:T(8,128)(2,1)} copy(bf16[4096,2048]{1,0:T(8,128)(2,1)} %convolution_convert_fusion) | data formatting | bytes 33554432 | tf_op jit(solution)/shard_map/convert_element_type | solution.py:46
  441.0 11.6 %copy.40 = bf16[256,8,16,256]{3,2,1,0:T(8,128)(2,1)S(1)} copy(bf16[256,8,16,256]{3,1,2,0:T(8,128)(2,1)} %bitcast.46) | data formatting | bytes 33554432
  452.6 6.7 %fusion.11 = f32[16,64,256]{2,0,1:T(8,128)} fusion(bf16[256,32,256]{2,1,0:T(8,128)(2,1)S(1)} %copy-done.24, bf16[16,256,64,32]{1,0,3,2:T(8,128)(2,1)S(1)} %bitcast.49), kind=kOutput, calls=%fused_computation.12 | convolution fusion | flops 4294967296 | bytes 22020096 | tf_op jit(solution)/shard_map/dot_general | solution.py:48
  459.6 102.4 %reduce-scatter.3.cloned.1.call-done = f32[16,4,256]{2,0,1:T(8,128)} async-done(((f32[16,64,256]{2,0,1:T(8,128)}), f32[16,4,256]{2,0,1:T(8,128)}) %reduce-scatter.3.cloned.1.call-update) | async-done | bytes 65552 | tf_op jit(solution)/shard_map/reduce_scatter | solution.py:52
  562.1 6.2 %reduce-scatter.5.cloned.1.call-done = f32[8,4,256]{2,0,1:T(8,128)} async-done(((f32[16,4,256]{2,0,1:T(8,128)}), f32[8,4,256]{2,0,1:T(8,128)}) %reduce-scatter.5.cloned.1.call-update) | async-done | bytes 32784 | tf_op jit(solution)/shard_map/reduce_scatter | solution.py:53
  (75 shorter events, 9.5 us)
Async XLA Ops:
  6.5 1.9 copy-start
  12.6 36.4 %collective-permute-start = (bf16[96,4096]{1,0:T(8,128)(2,1)}, bf16[96,4096]{1,0:T(8,128)(2,1)}, u32[]{:S(2)}, u32[]{:S(2)}) collective-permute-start(bf16[96,4096]{1,0:T(8,128)(2,1)} %bitcast.19), channel_id=1, source_target_pairs={{0,1},{1,2},{2,3},{3,4},{4,5},{5,6},{6,7},{7,8},{8,9},{9,10},{10,1... | collective-permute-start | bytes 2359304 | tf_op jit(solution)/shard_map/ppermute | solution.py:40
  43.0 262.9 %all-to-all-start = ((bf16[96,16,1024]{2,0,1:T(8,128)(2,1)}), bf16[96,16,1024]{2,0,1:T(8,128)(2,1)S(1)}, u32[]{:S(2)}, u32[]{:S(2)}) async-start(bf16[96,16,1024]{2,0,1:T(8,128)(2,1)} %copy.31), calls=%async_computation | async-start | bytes 6291456 | tf_op jit(solution)/shard_map/all_to_all | solution.py:30
  49.0 330.0 %all-gather.2.cloned.1.call-start = ((), (), s32[]{:S(2)}) async-start(), calls=%async_computation.3 | async-start | bytes 9437184 | tf_op jit(solution)/shard_map/all_gather | solution.py:31
  49.0 74.5 %collective-permute-start.1 = (bf16[96,4096]{1,0:T(8,128)(2,1)}, bf16[96,4096]{1,0:T(8,128)(2,1)S(1)}, u32[]{:S(2)}, u32[]{:S(2)}) collective-permute-start(bf16[96,4096]{1,0:T(8,128)(2,1)} %collective-permute-done), channel_id=1, source_target_pairs={{0,1},{1,2},{2,3},{3,4},{4,5},{5,6},{6,7},{7,8},{8,9},{9,10},{10,1... | collective-permute-start | bytes 2359304 | tf_op jit(solution)/shard_map/ppermute | solution.py:40
  51.0 75.3 %collective-permute-start.8 = (bf16[96,4096]{1,0:T(8,128)(2,1)}, bf16[96,4096]{1,0:T(8,128)(2,1)S(1)}, u32[]{:S(2)}, u32[]{:S(2)}) collective-permute-start(bf16[96,4096]{1,0:T(8,128)(2,1)} %bitcast.19), channel_id=1, source_target_pairs={{0,15},{1,0},{2,1},{3,2},{4,3},{5,4},{6,5},{7,6},{8,7},{9,8},{10,9... | collective-permute-start | bytes 2359304 | tf_op jit(solution)/shard_map/ppermute | solution.py:42
  123.5 35.9 %copy-start.5 = (bf16[96,4096]{1,0:T(8,128)(2,1)}, bf16[96,4096]{1,0:T(8,128)(2,1)S(1)}, u32[]{:S(2)}) copy-start(bf16[96,4096]{1,0:T(8,128)(2,1)S(1)} %collective-permute-done.1) | copy-start | bytes 2359300
  123.5 32.6 %collective-permute-start.2 = (bf16[96,4096]{1,0:T(8,128)(2,1)S(1)}, bf16[96,4096]{1,0:T(8,128)(2,1)S(1)}, u32[]{:S(2)}, u32[]{:S(2)}) collective-permute-start(bf16[96,4096]{1,0:T(8,128)(2,1)S(1)} %collective-permute-done.1), channel_id=1, source_target_pairs={{0,1},{1,2},{2,3},{3,4},{4,5},{5,6},{6,7},{7,8},{8,9},{9,10},{10,1... | collective-permute-start | bytes 2359304 | tf_op jit(solution)/shard_map/ppermute | solution.py:40
  126.3 0.9 copy-start.3
  127.2 32.1 %collective-permute-start.9 = (bf16[96,4096]{1,0:T(8,128)(2,1)S(1)}, bf16[96,4096]{1,0:T(8,128)(2,1)S(1)}, u32[]{:S(2)}, u32[]{:S(2)}) collective-permute-start(bf16[96,4096]{1,0:T(8,128)(2,1)S(1)} %collective-permute-done.8), channel_id=1, source_target_pairs={{0,15},{1,0},{2,1},{3,2},{4,3},{5,4},{6,5},{7,6},{8,7},{9,8},{10,9... | collective-permute-start | bytes 2359304 | tf_op jit(solution)/shard_map/ppermute | solution.py:42
  156.1 36.0 %copy-start.9 = (bf16[96,4096]{1,0:T(8,128)(2,1)}, bf16[96,4096]{1,0:T(8,128)(2,1)S(1)}, u32[]{:S(2)}) copy-start(bf16[96,4096]{1,0:T(8,128)(2,1)S(1)} %collective-permute-done.2) | copy-start | bytes 2359300
  156.1 21.0 %collective-permute-start.3 = (bf16[96,4096]{1,0:T(8,128)(2,1)S(1)}, bf16[96,4096]{1,0:T(8,128)(2,1)S(1)}, u32[]{:S(2)}, u32[]{:S(2)}) collective-permute-start(bf16[96,4096]{1,0:T(8,128)(2,1)S(1)} %collective-permute-done.2), channel_id=1, source_target_pairs={{0,1},{1,2},{2,3},{3,4},{4,5},{5,6},{6,7},{7,8},{8,9},{9,10},{10,1... | collective-permute-start | bytes 2359304 | tf_op jit(solution)/shard_map/ppermute | solution.py:40
  159.4 2.4 copy-start.7
  159.4 32.7 %collective-permute-start.10 = (bf16[96,4096]{1,0:T(8,128)(2,1)S(1)}, bf16[96,4096]{1,0:T(8,128)(2,1)S(1)}, u32[]{:S(2)}, u32[]{:S(2)}) collective-permute-start(bf16[96,4096]{1,0:T(8,128)(2,1)S(1)} %collective-permute-done.9), channel_id=1, source_target_pairs={{0,15},{1,0},{2,1},{3,2},{4,3},{5,4},{6,5},{7,6},{8,7},{9,8},{10,9... | collective-permute-start | bytes 2359304 | tf_op jit(solution)/shard_map/ppermute | solution.py:42
  177.1 93.8 %copy-start.15 = (bf16[96,4096]{1,0:T(8,128)(2,1)}, bf16[96,4096]{1,0:T(8,128)(2,1)S(1)}, u32[]{:S(2)}) copy-start(bf16[96,4096]{1,0:T(8,128)(2,1)S(1)} %collective-permute-done.3) | copy-start | bytes 2359300
  177.1 20.1 %collective-permute-start.4 = (bf16[96,4096]{1,0:T(8,128)(2,1)S(1)}, bf16[96,4096]{1,0:T(8,128)(2,1)S(1)}, u32[]{:S(2)}, u32[]{:S(2)}) collective-permute-start(bf16[96,4096]{1,0:T(8,128)(2,1)S(1)} %collective-permute-done.3), channel_id=1, source_target_pairs={{0,1},{1,2},{2,3},{3,4},{4,5},{5,6},{6,7},{7,8},{8,9},{9,10},{10,1... | collective-permute-start | bytes 2359304 | tf_op jit(solution)/shard_map/ppermute | solution.py:40
  192.1 0.9 copy-start.11
  192.1 43.0 %collective-permute-start.11 = (bf16[96,4096]{1,0:T(8,128)(2,1)S(1)}, bf16[96,4096]{1,0:T(8,128)(2,1)S(1)}, u32[]{:S(2)}, u32[]{:S(2)}) collective-permute-start(bf16[96,4096]{1,0:T(8,128)(2,1)S(1)} %collective-permute-done.10), channel_id=1, source_target_pairs={{0,15},{1,0},{2,1},{3,2},{4,3},{5,4},{6,5},{7,6},{8,7},{9,8},{10,9... | collective-permute-start | bytes 2359304 | tf_op jit(solution)/shard_map/ppermute | solution.py:42
  197.2 73.7 %copy-start.17 = (bf16[96,4096]{1,0:T(8,128)(2,1)}, bf16[96,4096]{1,0:T(8,128)(2,1)S(1)}, u32[]{:S(2)}) copy-start(bf16[96,4096]{1,0:T(8,128)(2,1)S(1)} %collective-permute-done.4) | copy-start | bytes 2359300
  197.2 54.6 %collective-permute-start.5 = (bf16[96,4096]{1,0:T(8,128)(2,1)S(1)}, bf16[96,4096]{1,0:T(8,128)(2,1)S(1)}, u32[]{:S(2)}, u32[]{:S(2)}) collective-permute-start(bf16[96,4096]{1,0:T(8,128)(2,1)S(1)} %collective-permute-done.4), channel_id=1, source_target_pairs={{0,1},{1,2},{2,3},{3,4},{4,5},{5,6},{6,7},{7,8},{8,9},{9,10},{10,1... | collective-permute-start | bytes 2359304 | tf_op jit(solution)/shard_map/ppermute | solution.py:40
  235.0 0.9 copy-start.13
  235.9 35.0 %collective-permute-start.12 = (bf16[96,4096]{1,0:T(8,128)(2,1)S(1)}, bf16[96,4096]{1,0:T(8,128)(2,1)}, u32[]{:S(2)}, u32[]{:S(2)}) collective-permute-start(bf16[96,4096]{1,0:T(8,128)(2,1)S(1)} %collective-permute-done.11), channel_id=1, source_target_pairs={{0,15},{1,0},{2,1},{3,2},{4,3},{5,4},{6,5},{7,6},{8,7},{9,8},{10,9... | collective-permute-start | bytes 2359304 | tf_op jit(solution)/shard_map/ppermute | solution.py:42
  251.7 19.2 %copy-start.19 = (bf16[96,4096]{1,0:T(8,128)(2,1)}, bf16[96,4096]{1,0:T(8,128)(2,1)S(1)}, u32[]{:S(2)}) copy-start(bf16[96,4096]{1,0:T(8,128)(2,1)S(1)} %collective-permute-done.5) | copy-start | bytes 2359300
  251.7 19.2 %collective-permute-start.6 = (bf16[96,4096]{1,0:T(8,128)(2,1)S(1)}, bf16[96,4096]{1,0:T(8,128)(2,1)}, u32[]{:S(2)}, u32[]{:S(2)}) collective-permute-start(bf16[96,4096]{1,0:T(8,128)(2,1)S(1)} %collective-permute-done.5), channel_id=1, source_target_pairs={{0,1},{1,2},{2,3},{3,4},{4,5},{5,6},{6,7},{7,8},{8,9},{9,10},{10,1... | collective-permute-start | bytes 2359304 | tf_op jit(solution)/shard_map/ppermute | solution.py:40
  270.9 34.9 %collective-permute-start.13 = (bf16[96,4096]{1,0:T(8,128)(2,1)}, bf16[96,4096]{1,0:T(8,128)(2,1)}, u32[]{:S(2)}, u32[]{:S(2)}) collective-permute-start(bf16[96,4096]{1,0:T(8,128)(2,1)} %collective-permute-done.12), channel_id=1, source_target_pairs={{0,15},{1,0},{2,1},{3,2},{4,3},{5,4},{6,5},{7,6},{8,7},{9,8},{10,9... | collective-permute-start | bytes 2359304 | tf_op jit(solution)/shard_map/ppermute | solution.py:42
  271.0 51.1 %collective-permute-start.7 = (bf16[96,4096]{1,0:T(8,128)(2,1)}, bf16[96,4096]{1,0:T(8,128)(2,1)}, u32[]{:S(2)}, u32[]{:S(2)}) collective-permute-start(bf16[96,4096]{1,0:T(8,128)(2,1)} %collective-permute-done.6), channel_id=1, source_target_pairs={{0,1},{1,2},{2,3},{3,4},{4,5},{5,6},{6,7},{7,8},{8,9},{9,10},{10,1... | collective-permute-start | bytes 2359304 | tf_op jit(solution)/shard_map/ppermute | solution.py:40
  305.9 47.8 %collective-permute-start.14 = (bf16[96,4096]{1,0:T(8,128)(2,1)}, bf16[96,4096]{1,0:T(8,128)(2,1)}, u32[]{:S(2)}, u32[]{:S(2)}) collective-permute-start(bf16[96,4096]{1,0:T(8,128)(2,1)} %collective-permute-done.13), channel_id=1, source_target_pairs={{0,15},{1,0},{2,1},{3,2},{4,3},{5,4},{6,5},{7,6},{8,7},{9,8},{10,9... | collective-permute-start | bytes 2359304 | tf_op jit(solution)/shard_map/ppermute | solution.py:42
  305.9 1.6 copy-start.2
  307.6 55.2 %copy-start.10 = (bf16[96,4096]{1,0:T(8,128)(2,1)S(1)}, bf16[96,4096]{1,0:T(8,128)(2,1)}, u32[]{:S(2)}) copy-start(bf16[96,4096]{1,0:T(8,128)(2,1)} %copy-done.9) | copy-start | bytes 2359300
  307.6 56.2 %copy-start.6 = (bf16[96,4096]{1,0:T(8,128)(2,1)S(1)}, bf16[96,4096]{1,0:T(8,128)(2,1)}, u32[]{:S(2)}) copy-start(bf16[96,4096]{1,0:T(8,128)(2,1)} %copy-done.5) | copy-start | bytes 2359300
  307.6 61.3 %copy-start.4 = (bf16[96,4096]{1,0:T(8,128)(2,1)S(1)}, bf16[96,4096]{1,0:T(8,128)(2,1)}, u32[]{:S(2)}) copy-start(bf16[96,4096]{1,0:T(8,128)(2,1)} %copy-done.3) | copy-start | bytes 2359300
  307.6 62.2 %copy-start.8 = (bf16[96,4096]{1,0:T(8,128)(2,1)S(1)}, bf16[96,4096]{1,0:T(8,128)(2,1)}, u32[]{:S(2)}) copy-start(bf16[96,4096]{1,0:T(8,128)(2,1)} %copy-done.7) | copy-start | bytes 2359300
  307.6 254.4 %reduce-scatter.3.cloned.1.call-start = ((), (), s32[]{:S(2)}) async-start(), calls=%async_computation.4 | async-start | bytes 1114112 | tf_op jit(solution)/shard_map/reduce_scatter | solution.py:52
  307.8 52.1 %copy-start.20 = (bf16[96,4096]{1,0:T(8,128)(2,1)S(1)}, bf16[96,4096]{1,0:T(8,128)(2,1)}, u32[]{:S(2)}) copy-start(bf16[96,4096]{1,0:T(8,128)(2,1)} %copy-done.19) | copy-start | bytes 2359300
  307.8 53.0 %copy-start.18 = (bf16[96,4096]{1,0:T(8,128)(2,1)S(1)}, bf16[96,4096]{1,0:T(8,128)(2,1)}, u32[]{:S(2)}) copy-start(bf16[96,4096]{1,0:T(8,128)(2,1)} %copy-done.17) | copy-start | bytes 2359300
  307.8 54.0 %copy-start.16 = (bf16[96,4096]{1,0:T(8,128)(2,1)S(1)}, bf16[96,4096]{1,0:T(8,128)(2,1)}, u32[]{:S(2)}) copy-start(bf16[96,4096]{1,0:T(8,128)(2,1)} %copy-done.15) | copy-start | bytes 2359300
  307.9 62.9 %copy-start.12 = (bf16[96,4096]{1,0:T(8,128)(2,1)S(1)}, bf16[96,4096]{1,0:T(8,128)(2,1)}, u32[]{:S(2)}) copy-start(bf16[96,4096]{1,0:T(8,128)(2,1)} %copy-done.11) | copy-start | bytes 2359300
  307.9 63.9 %copy-start.14 = (bf16[96,4096]{1,0:T(8,128)(2,1)S(1)}, bf16[96,4096]{1,0:T(8,128)(2,1)}, u32[]{:S(2)}) copy-start(bf16[96,4096]{1,0:T(8,128)(2,1)} %copy-done.13) | copy-start | bytes 2359300
  441.0 11.6 %copy-start.24 = (bf16[256,32,256]{2,1,0:T(8,128)(2,1)S(1)}, bf16[256,32,256]{2,1,0:T(8,128)(2,1)}, u32[]{:S(2)}) copy-start(bf16[256,32,256]{2,1,0:T(8,128)(2,1)} %param.14) | copy-start | bytes 12582916
  441.0 128.8 %copy-start.1 = (f32[96,16,512]{2,1,0:T(8,128)S(1)}, f32[96,16,512]{2,1,0:T(8,128)}, u32[]{:S(2)}) copy-start(f32[96,16,512]{2,1,0:T(8,128)} %param.11) | copy-start | bytes 9437188
  452.5 6.9 %copy-start.21 = (f32[16]{0:T(128)S(1)}, f32[16]{0:T(128)}, u32[]{:S(2)}) copy-start(f32[16]{0:T(128)} %param.17) | copy-start | bytes 196
  452.5 109.4 %copy-start.22 = (f32[4]{0:T(128)S(1)}, f32[4]{0:T(128)}, u32[]{:S(2)}) copy-start(f32[4]{0:T(128)} %param.16) | copy-start | bytes 52
  452.6 109.4 %copy-start.23 = (f32[8]{0:T(128)S(1)}, f32[8]{0:T(128)}, u32[]{:S(2)}) copy-start(f32[8]{0:T(128)} %param.15) | copy-start | bytes 100
  459.3 108.9 %reduce-scatter.5.cloned.1.call-start = ((), (), s32[]{:S(2)}) async-start(), calls=%async_computation.5 | async-start | bytes 98304 | tf_op jit(solution)/shard_map/reduce_scatter | solution.py:53
Sparse Core Ops, SparseCore 0:
  307.7 43.3 all-gather.1
  459.5 102.4 reduce-scatter.2
  564.1 4.0 reduce-scatter.4
